TPU v7x, 32 devices: a whole 2x2x4 slice. The times are simulated.
32 devices in a mesh: groups: 2 (over y), ctx: 8 (over z, core), tp: 2 (over x), section: 1.
Axes of the slice: x: 2, y: 2, z: 4, core: 2. Of those that a mesh axis runs over, the one named last changes fastest.
Arguments:
- doc_lengths: int32 [8], P('groups'), parts along dimension 0, may hold values from 1 to 1024, 2048 in all
- queries: bfloat16 [1, 4096, 2048], P('section', ('groups', 'ctx'), 'tp'), parts along dimension 1, may hold values from -30 to 30
- keys: bfloat16 [1, 4096, 1024], P('section', ('groups', 'ctx'), 'tp'), parts along dimension 1, may hold values from -30 to 30
- values: bfloat16 [1, 4096, 1024], P('section', ('groups', 'ctx'), 'tp'), parts along dimension 1, may hold values from -6 to 6
- out_grad: bfloat16 [1, 4096, 2048], P('section', ('groups', 'ctx'), 'tp'), parts along dimension 1, may hold values from -6 to 6
Outputs:
- attn_out: bfloat16 [1, 4096, 2048], P('section', ('groups', 'ctx'), 'tp'), parts along dimension 1
- grad_queries: bfloat16 [1, 4096, 2048], P('section', ('groups', 'ctx'), 'tp'), parts along dimension 1
- grad_keys: bfloat16 [1, 4096, 1024], P('section', ('groups', 'ctx'), 'tp'), parts along dimension 1
- grad_values: bfloat16 [1, 4096, 1024], P('section', ('groups', 'ctx'), 'tp'), parts along dimension 1
There are 2 independent parts, one for each index of `groups`. A program takes and returns all parts, laid end to end along the dimension named above; each array names one. Nothing has to cross between parts.
All inputs are finite; a program needn't handle non-finite values.
Results may differ from a plain program's by a relative error of at most 0.02.
Values may be sent and summed in bfloat16 or wider, within the bound.
A program may use at most 64 MiB of HBM per device.

v0:
```python
import functools

import jax
import jax.numpy as jnp
from jax import lax
from jax.experimental import pallas as pl
from jax.experimental.pallas import tpu as pltpu
from jax.sharding import PartitionSpec as P

HEAD_DIM = 256
LOOKBACK_SIZE = 2048
F32 = jnp.float32
BF16 = jnp.bfloat16
CONTRACT_LAST = (((1,), (1,)), ((), ()))
CONTRACT_FIRST = (((0,), (0,)), ((), ()))


def kernel(
    n, hops, docs_ref, q_ref, k_ref, v_ref, g_ref, o_ref, dq_ref, dk_ref, dv_ref,
    win, q2, g2, s_ref, p_ref, dp_ref, acc, sbuf, cbuf, rsib, rchain,
    fs, fr, ss, sr, bs, br, cs, cr,
):
    tok = q_ref.shape[0]
    kv = k_ref.shape[1] // HEAD_DIM
    group = q_ref.shape[1] // k_ref.shape[1]
    cols = group * tok
    slots = 2 * hops + 1
    scale = HEAD_DIM ** (-0.5)
    d = lax.axis_index("ctx")
    c = lax.rem(d, 2)
    up = lax.rem(d + 2, n)
    down = lax.rem(d + n - 2, n)
    sibling = d + 1 - 2 * c

    def remote(src, dst, send, recv, device):
        return pltpu.make_async_remote_copy(
            src_ref=src, dst_ref=dst, send_sem=send, recv_sem=recv,
            device_id={"ctx": device}, device_id_type=pl.DeviceIdType.MESH,
        )

    def fwd(x, t):
        return remote(win.at[x, 2 * t - 2], win.at[x, 2 * t], fs.at[x, t - 1], fr.at[x, t - 1], up)

    def sib(x, u):
        return remote(win.at[x, 2 * u + 2 * c], win.at[x, 2 * u + 1], ss.at[x, u], sr.at[x, u], sibling)

    def bsib(x, u):
        return remote(sbuf.at[x, u], rsib.at[x, u], bs.at[x, u], br.at[x, u], sibling)

    def chain(x, t):
        return remote(cbuf.at[x, t - 1], rchain.at[x, t - 1], cs.at[x, t - 1], cr.at[x, t - 1], down)

    def start_own(x):
        @pl.when(d + 2 < n)
        def _():
            fwd(x, 1).start()

        @pl.when(c == 0)
        def _():
            sib(x, 0).start()

    def arrive(x, t):
        @pl.when(d >= 2 * t)
        def _():
            fwd(x, t).wait_recv()
            if t < hops:
                @pl.when(d + 2 < n)
                def _():
                    fwd(x, t + 1).start()

                @pl.when(c == 0)
                def _():
                    sib(x, t).start()

            @pl.when(c == 1)
            def _():
                sib(x, t - 1).start()

    def arrive_sib(x):
        for u in range(hops):
            @pl.when(d >= 2 * u + 1)
            def _():
                sib(x, u).wait_recv()

    def send_odd(x, u, part):
        sbuf[x, u] = part.astype(BF16)

        @pl.when(d >= 2 * u + 1)
        def _():
            bsib(x, u).start()

    def chain_step(x, t, out_ref, lo):
        @pl.when(d >= 2 * t)
        def _():
            if t < hops:
                @pl.when(c == 0)
                def _():
                    bsib(x, t).wait_recv()
                    acc[x, t] += rsib[x, t].astype(F32)
            if t >= 1:
                @pl.when(c == 1)
                def _():
                    bsib(x, t - 1).wait_recv()
                    acc[x, t] += rsib[x, t - 1].astype(F32)
            if t < hops:
                @pl.when(d + 2 < n)
                def _():
                    chain(x, t + 1).wait_recv()
                    acc[x, t] += rchain[x, t].astype(F32)
            if t > 0:
                cbuf[x, t - 1] = acc[x, t].astype(BF16)
                chain(x, t).start()
            else:
                out_ref[:, lo : lo + HEAD_DIM] = acc[x, t].astype(BF16)

    def finish_sends(x):
        for t in range(1, hops + 1):
            @pl.when((d + 2 < n) & (d >= 2 * t - 2))
            def _():
                fwd(x, t).wait_send()

            @pl.when(d >= 2 * t)
            def _():
                chain(x, t).wait_send()
        for u in range(hops):
            @pl.when(d >= 2 * u + 2 * c)
            def _():
                sib(x, u).wait_send()

            @pl.when(d >= 2 * u + 1)
            def _():
                bsib(x, u).wait_send()

    barrier = pltpu.get_barrier_semaphore()
    for other in (up, down, sibling):
        pl.semaphore_signal(
            barrier, inc=1, device_id={"ctx": other}, device_id_type=pl.DeviceIdType.MESH
        )
    for h in range(kv):
        lo = h * HEAD_DIM
        win[2 * h, 0] = k_ref[:, lo : lo + HEAD_DIM]
        win[2 * h + 1, 0] = v_ref[:, lo : lo + HEAD_DIM]
    pl.semaphore_wait(barrier, 3)
    start_own(0)
    start_own(1)

    for r in range(1, slots):
        @pl.when(d < r)
        def _():
            for x in range(2 * kv):
                win[x, r] = jnp.zeros((tok, HEAD_DIM), BF16)
    for h in range(kv):
        for e in range(group):
            lo = (h * group + e) * HEAD_DIM
            q2[h, e * tok : (e + 1) * tok, :] = q_ref[:, lo : lo + HEAD_DIM]
            g2[h, e * tok : (e + 1) * tok, :] = g_ref[:, lo : lo + HEAD_DIM]

    qpos = d * tok + lax.rem(lax.broadcasted_iota(jnp.int32, (1, cols), 1), tok)
    low = jnp.zeros((1, cols), jnp.int32)
    offset = jnp.int32(0)
    for i in range(docs_ref.shape[0]):
        low = jnp.where(offset <= qpos, jnp.maximum(low, offset), low)
        offset = offset + docs_ref[i]
    low = jnp.maximum(low, qpos - (LOOKBACK_SIZE - 1))

    def rows(r):
        return pl.ds(pl.multiple_of(r * tok, tok), tok)

    def stage_probs(h):
        x = 2 * h

        def score(r, top):
            s = lax.dot_general(win[x, r], q2[h], CONTRACT_LAST, preferred_element_type=F32) * scale
            kpos = (d - r) * tok + lax.broadcasted_iota(jnp.int32, (tok, 1), 0)
            s = jnp.where((kpos <= qpos) & (kpos >= low), s, -1e30)
            s_ref[rows(r), :] = s
            return jnp.maximum(top, jnp.max(s, axis=0, keepdims=True))

        top = lax.fori_loop(0, slots, score, jnp.full((1, cols), -1e30, F32))

        def expo(r, total):
            e = jnp.exp(s_ref[rows(r), :] - top)
            s_ref[rows(r), :] = e
            return total + jnp.sum(e, axis=0, keepdims=True)

        total = lax.fori_loop(0, slots, expo, jnp.zeros((1, cols), F32))
        inv = 1.0 / total

        def norm(r, carry):
            prob = s_ref[rows(r), :] * inv
            s_ref[rows(r), :] = prob
            p_ref[rows(r), :] = prob.astype(BF16)
            return carry

        lax.fori_loop(0, slots, norm, 0)

    def part_sums(x, lhs, rhs):
        order = list(range(slots - 2, 0, -2)) + list(range(slots - 1, -1, -2))
        for r in order:
            part = jnp.dot(lhs[r * tok : (r + 1) * tok, :], rhs, preferred_element_type=F32)
            if r % 2:
                send_odd(x, r // 2, part)
            else:
                acc[x, r // 2] = part

    def stage_scores(h):
        x = 2 * h

        def dprob(r, delta):
            dp = lax.dot_general(win[x + 1, r], g2[h], CONTRACT_LAST, preferred_element_type=F32)
            dp_ref[rows(r), :] = dp
            return delta + jnp.sum(dp * s_ref[rows(r), :], axis=0, keepdims=True)

        delta = lax.fori_loop(0, slots, dprob, jnp.zeros((1, cols), F32))

        def dscore(r, carry):
            ds = s_ref[rows(r), :] * (dp_ref[rows(r), :] - delta) * scale
            d_ref = dp_ref
            d_ref[rows(r), :] = ds
            return carry

        lax.fori_loop(0, slots, dscore, 0)

    def emit(ref, h, weights, source):
        whole = source.reshape(slots * tok, HEAD_DIM)
        res = lax.dot_general(weights, whole, CONTRACT_FIRST, preferred_element_type=F32)
        for e in range(group):
            lo = (h * group + e) * HEAD_DIM
            ref[:, lo : lo + HEAD_DIM] = res[e * tok : (e + 1) * tok, :].astype(BF16)

    for h in range(kv):
        lo = h * HEAD_DIM
        x = 2 * h
        for t in range(1, hops + 1):
            arrive(x, t)
            arrive(x + 1, t)
            if t == 1 and h + 1 < kv:
                start_own(x + 2)
                start_own(x + 3)
        arrive_sib(x)
        stage_probs(h)
        part_sums(x + 1, p_ref, g2[h])
        arrive_sib(x + 1)
        chain_step(x + 1, hops, dv_ref, lo)
        stage_scores(h)
        emit(o_ref, h, p_ref[...], win[x + 1])
        p_ref[...] = dp_ref[...].astype(BF16)
        part_sums(x, p_ref, q2[h])
        chain_step(x, hops, dk_ref, lo)
        emit(dq_ref, h, p_ref[...], win[x])
        for t in range(hops - 1, -1, -1):
            chain_step(x + 1, t, dv_ref, lo)
            chain_step(x, t, dk_ref, lo)
    for x in range(2 * kv):
        finish_sends(x)


def body(n, doc_lengths, queries, keys, values, out_grad):
    tok, width = keys.shape[1:]
    kv = width // HEAD_DIM
    cols = queries.shape[2] // width * tok
    reach = -(-min(LOOKBACK_SIZE, tok * n // 2) // tok)
    hops = -(-reach // 2)
    slots = 2 * hops + 1
    spec = pl.BlockSpec(memory_space=pltpu.VMEM)
    tile = (tok, HEAD_DIM)
    chunks = 2 * kv
    dma = pltpu.SemaphoreType.DMA((chunks, hops))
    out = pl.pallas_call(
        functools.partial(kernel, n, hops),
        out_shape=(
            jax.ShapeDtypeStruct(queries.shape[1:], BF16),
            jax.ShapeDtypeStruct(queries.shape[1:], BF16),
            jax.ShapeDtypeStruct(keys.shape[1:], BF16),
            jax.ShapeDtypeStruct(keys.shape[1:], BF16),
        ),
        in_specs=[pl.BlockSpec(memory_space=pltpu.SMEM)] + [spec] * 4,
        out_specs=(spec,) * 4,
        scratch_shapes=[
            pltpu.VMEM((chunks, slots) + tile, BF16),
            pltpu.VMEM((kv, cols, HEAD_DIM), BF16),
            pltpu.VMEM((kv, cols, HEAD_DIM), BF16),
            pltpu.VMEM((slots * tok, cols), F32),
            pltpu.VMEM((slots * tok, cols), BF16),
            pltpu.VMEM((slots * tok, cols), F32),
            pltpu.VMEM((chunks, hops + 1) + tile, F32),
            pltpu.VMEM((chunks, hops) + tile, BF16),
            pltpu.VMEM((chunks, hops) + tile, BF16),
            pltpu.VMEM((chunks, hops) + tile, BF16),
            pltpu.VMEM((chunks, hops) + tile, BF16),
        ]
        + [dma] * 8,
        compiler_params=pltpu.CompilerParams(
            collective_id=0, has_side_effects=True, vmem_limit_bytes=50 * 1024 * 1024
        ),
    )(doc_lengths, queries[0], keys[0], values[0], out_grad[0])
    return tuple(o[None] for o in out)


def solution(mesh):
    spec = P("section", ("groups", "ctx"), "tp")
    return jax.shard_map(
        functools.partial(body, mesh.shape["ctx"]),
        mesh=mesh,
        in_specs=(P("groups"),) + (spec,) * 4,
        out_specs=(spec,) * 4,
        check_vma=False,
    )
```

profile of v0, /device:TPU:0, one launch (start us, length us, event | category | flops | bytes accessed | tf_op | source)
XLA Modules:
  0.0 69.5 jit_solution(12796254687370103403)
XLA Ops:
  0.6 0.0 copy-start.4
  0.6 0.6 copy-done.4
  1.3 0.0 copy-start
  1.3 1.0 %copy-done = bf16[1,256,1024]{2,1,0:T(8,128)(2,1)S(1)} copy-done((bf16[1,256,1024]{2,1,0:T(8,128)(2,1)S(1)}, bf16[1,256,1024]{2,1,0:T(8,128)(2,1)}, u32[]{:S(2)}) %copy-start) | copy-done | bytes 524312
  2.3 0.0 copy-start.1
  2.3 1.0 %copy-done.1 = bf16[1,256,1024]{2,1,0:T(8,128)(2,1)S(1)} copy-done((bf16[1,256,1024]{2,1,0:T(8,128)(2,1)S(1)}, bf16[1,256,1024]{2,1,0:T(8,128)(2,1)}, u32[]{:S(2)}) %copy-start.1) | copy-done | bytes 524312
  3.4 0.0 copy-start.2
  3.4 0.9 %copy-done.2 = bf16[1,256,512]{2,1,0:T(8,128)(2,1)S(1)} copy-done((bf16[1,256,512]{2,1,0:T(8,128)(2,1)S(1)}, bf16[1,256,512]{2,1,0:T(8,128)(2,1)}, u32[]{:S(2)}) %copy-start.2) | copy-done | bytes 262168
  4.3 0.0 copy-start.3
  4.3 0.9 %copy-done.3 = bf16[1,256,512]{2,1,0:T(8,128)(2,1)S(1)} copy-done((bf16[1,256,512]{2,1,0:T(8,128)(2,1)S(1)}, bf16[1,256,512]{2,1,0:T(8,128)(2,1)}, u32[]{:S(2)}) %copy-start.3) | copy-done | bytes 262168
  5.3 61.3 %shard_map.84 = (bf16[256,1024]{1,0:T(8,128)(2,1)S(1)}, bf16[256,1024]{1,0:T(8,128)(2,1)S(1)}, bf16[256,512]{1,0:T(8,128)(2,1)S(1)}, bf16[256,512]{1,0:T(8,128)(2,1)S(1)}) custom-call(s32[4]{0:T(128)S(1)} %copy-done.4, bf16[256,1024]{1,0:T(8,128)(2,1)S(1)} %bitcast.8, bf16[256,512]{1,0:T(8,128)(2,1)S(1)} %bitcast.14, bf16[256,512]{1,0:T(8,128)(2,1)S(1)} %bitcast.15, ...), custom_call_target="tpu_custom_call" | custom-call | tf_op jit(solution)/shard_map/pallas_call | solution.py:269
  66.5 0.8 %copy.13 = bf16[1,256,1024]{2,1,0:T(8,128)(2,1)} copy(bf16[1,256,1024]{2,1,0:T(8,128)(2,1)S(1)} %bitcast.11) | data formatting | bytes 1048576
  67.3 0.8 %copy.14 = bf16[1,256,1024]{2,1,0:T(8,128)(2,1)} copy(bf16[1,256,1024]{2,1,0:T(8,128)(2,1)S(1)} %bitcast.10) | data formatting | bytes 1048576
  68.1 0.7 %copy.15 = bf16[1,256,512]{2,1,0:T(8,128)(2,1)} copy(bf16[1,256,512]{2,1,0:T(8,128)(2,1)S(1)} %bitcast.13) | data formatting | bytes 524288
  68.8 0.7 %copy.16 = bf16[1,256,512]{2,1,0:T(8,128)(2,1)} copy(bf16[1,256,512]{2,1,0:T(8,128)(2,1)S(1)} %bitcast.12) | data formatting | bytes 524288
Async XLA Ops:
  0.6 0.7 copy-start.4
  1.3 1.0 %copy-start = (bf16[1,256,1024]{2,1,0:T(8,128)(2,1)S(1)}, bf16[1,256,1024]{2,1,0:T(8,128)(2,1)}, u32[]{:S(2)}) copy-start(bf16[1,256,1024]{2,1,0:T(8,128)(2,1)} %param.6) | copy-start | bytes 1572868
  2.3 1.0 %copy-start.1 = (bf16[1,256,1024]{2,1,0:T(8,128)(2,1)S(1)}, bf16[1,256,1024]{2,1,0:T(8,128)(2,1)}, u32[]{:S(2)}) copy-start(bf16[1,256,1024]{2,1,0:T(8,128)(2,1)} %param.9) | copy-start | bytes 1572868
  3.4 0.9 %copy-start.2 = (bf16[1,256,512]{2,1,0:T(8,128)(2,1)S(1)}, bf16[1,256,512]{2,1,0:T(8,128)(2,1)}, u32[]{:S(2)}) copy-start(bf16[1,256,512]{2,1,0:T(8,128)(2,1)} %param.7) | copy-start | bytes 786436
  4.3 0.9 %copy-start.3 = (bf16[1,256,512]{2,1,0:T(8,128)(2,1)S(1)}, bf16[1,256,512]{2,1,0:T(8,128)(2,1)}, u32[]{:S(2)}) copy-start(bf16[1,256,512]{2,1,0:T(8,128)(2,1)} %param.8) | copy-start | bytes 786436
where the time goes:
time: 69.8 us; the launch traced here: 69.5 us
  Pallas kernels  61.3 us (88%)
  local copies, waits for them, and re-layouts  7.62 us (11%)
    pallas_call x1, Pallas kernels, body(): pl.pallas_call(functools.partial(kernel, n, hops), out_shape=(jax.ShapeDt...  61.3 us
    unnamed x14, local copies, waits for them, and re-layouts  7.62 us

commit v1 on v0

--- a/solution.py
+++ b/solution.py
@@ -17,8 +17,8 @@
 
 def kernel(
     n, hops, docs_ref, q_ref, k_ref, v_ref, g_ref, o_ref, dq_ref, dk_ref, dv_ref,
-    win, q2, g2, s_ref, p_ref, dp_ref, acc, sbuf, cbuf, rsib, rchain,
-    fs, fr, ss, sr, bs, br, cs, cr,
+    win, q2, g2, s_ref, p_ref, dp_ref, ds_ref, acc, sbuf, cbuf, rsib, rchain,
+    lk, lq, lg, fs, fr, ss, sr, bs, br, cs, cr,
 ):
     tok = q_ref.shape[0]
     kv = k_ref.shape[1] // HEAD_DIM
@@ -50,7 +50,20 @@
     def chain(x, t):
         return remote(cbuf.at[x, t - 1], rchain.at[x, t - 1], cs.at[x, t - 1], cr.at[x, t - 1], down)
 
+    def load(x):
+        lo = x // 2 * HEAD_DIM
+        source = v_ref if x % 2 else k_ref
+        return pltpu.make_async_copy(source.at[:, lo : lo + HEAD_DIM], win.at[x, 0], lk.at[x])
+
+    def load_rows(source, target, sem, h, e):
+        lo = (h * group + e) * HEAD_DIM
+        return pltpu.make_async_copy(
+            source.at[:, lo : lo + HEAD_DIM], target.at[h, e * tok : (e + 1) * tok, :], sem.at[h, e]
+        )
+
     def start_own(x):
+        load(x).wait()
+
         @pl.when(d + 2 < n)
         def _():
             fwd(x, 1).start()
@@ -137,23 +150,25 @@
             barrier, inc=1, device_id={"ctx": other}, device_id_type=pl.DeviceIdType.MESH
         )
     for h in range(kv):
-        lo = h * HEAD_DIM
-        win[2 * h, 0] = k_ref[:, lo : lo + HEAD_DIM]
-        win[2 * h + 1, 0] = v_ref[:, lo : lo + HEAD_DIM]
+        load(2 * h).start()
+        for e in range(group):
+            load_rows(q_ref, q2, lq, h, e).start()
+        load(2 * h + 1).start()
+        for e in range(group):
+            load_rows(g_ref, g2, lg, h, e).start()
     pl.semaphore_wait(barrier, 3)
     start_own(0)
-    start_own(1)
-
+
+    for h in range(kv):
+        for e in range(group):
+            load_rows(q_ref, q2, lq, h, e).wait()
+            load_rows(g_ref, g2, lg, h, e).wait()
+        q2[h] = q2[h] * BF16(scale)
     for r in range(1, slots):
         @pl.when(d < r)
         def _():
             for x in range(2 * kv):
                 win[x, r] = jnp.zeros((tok, HEAD_DIM), BF16)
-    for h in range(kv):
-        for e in range(group):
-            lo = (h * group + e) * HEAD_DIM
-            q2[h, e * tok : (e + 1) * tok, :] = q_ref[:, lo : lo + HEAD_DIM]
-            g2[h, e * tok : (e + 1) * tok, :] = g_ref[:, lo : lo + HEAD_DIM]
 
     qpos = d * tok + lax.rem(lax.broadcasted_iota(jnp.int32, (1, cols), 1), tok)
     low = jnp.zeros((1, cols), jnp.int32)
@@ -164,66 +179,53 @@
     low = jnp.maximum(low, qpos - (LOOKBACK_SIZE - 1))
 
     def rows(r):
-        return pl.ds(pl.multiple_of(r * tok, tok), tok)
-
-    def stage_probs(h):
-        x = 2 * h
-
-        def score(r, top):
-            s = lax.dot_general(win[x, r], q2[h], CONTRACT_LAST, preferred_element_type=F32) * scale
-            kpos = (d - r) * tok + lax.broadcasted_iota(jnp.int32, (tok, 1), 0)
-            s = jnp.where((kpos <= qpos) & (kpos >= low), s, -1e30)
-            s_ref[rows(r), :] = s
-            return jnp.maximum(top, jnp.max(s, axis=0, keepdims=True))
-
-        top = lax.fori_loop(0, slots, score, jnp.full((1, cols), -1e30, F32))
-
-        def expo(r, total):
+        return pl.ds(r * tok, tok)
+
+    def score(h, r, top):
+        s = lax.dot_general(win[2 * h, r], q2[h], CONTRACT_LAST, preferred_element_type=F32)
+        kpos = (d - r) * tok + lax.broadcasted_iota(jnp.int32, (tok, 1), 0)
+        allowed = kpos >= low
+        if r == 0:
+            allowed = allowed & (kpos <= qpos)
+        s = jnp.where(allowed, s, -1e30)
+        s_ref[rows(r), :] = s
+        return jnp.maximum(top, jnp.max(s, axis=0, keepdims=True))
+
+    def probs(top):
+        total = jnp.zeros((1, cols), F32)
+        for r in range(slots):
             e = jnp.exp(s_ref[rows(r), :] - top)
             s_ref[rows(r), :] = e
-            return total + jnp.sum(e, axis=0, keepdims=True)
-
-        total = lax.fori_loop(0, slots, expo, jnp.zeros((1, cols), F32))
+            total = total + jnp.sum(e, axis=0, keepdims=True)
         inv = 1.0 / total
-
-        def norm(r, carry):
+        for r in range(slots):
             prob = s_ref[rows(r), :] * inv
             s_ref[rows(r), :] = prob
             p_ref[rows(r), :] = prob.astype(BF16)
-            return carry
-
-        lax.fori_loop(0, slots, norm, 0)
 
     def part_sums(x, lhs, rhs):
         order = list(range(slots - 2, 0, -2)) + list(range(slots - 1, -1, -2))
         for r in order:
-            part = jnp.dot(lhs[r * tok : (r + 1) * tok, :], rhs, preferred_element_type=F32)
+            part = jnp.dot(lhs[rows(r), :], rhs, preferred_element_type=F32)
             if r % 2:
                 send_odd(x, r // 2, part)
             else:
                 acc[x, r // 2] = part
 
-    def stage_scores(h):
-        x = 2 * h
-
-        def dprob(r, delta):
-            dp = lax.dot_general(win[x + 1, r], g2[h], CONTRACT_LAST, preferred_element_type=F32)
+    def dscores(h):
+        delta = jnp.zeros((1, cols), F32)
+        for r in range(slots):
+            dp = lax.dot_general(win[2 * h + 1, r], g2[h], CONTRACT_LAST, preferred_element_type=F32)
             dp_ref[rows(r), :] = dp
-            return delta + jnp.sum(dp * s_ref[rows(r), :], axis=0, keepdims=True)
-
-        delta = lax.fori_loop(0, slots, dprob, jnp.zeros((1, cols), F32))
-
-        def dscore(r, carry):
-            ds = s_ref[rows(r), :] * (dp_ref[rows(r), :] - delta) * scale
-            d_ref = dp_ref
-            d_ref[rows(r), :] = ds
-            return carry
-
-        lax.fori_loop(0, slots, dscore, 0)
-
-    def emit(ref, h, weights, source):
+            delta = delta + jnp.sum(dp * s_ref[rows(r), :], axis=0, keepdims=True)
+        for r in range(slots):
+            ds_ref[rows(r), :] = (s_ref[rows(r), :] * (dp_ref[rows(r), :] - delta)).astype(BF16)
+
+    def emit(ref, h, weights, source, factor):
         whole = source.reshape(slots * tok, HEAD_DIM)
         res = lax.dot_general(weights, whole, CONTRACT_FIRST, preferred_element_type=F32)
+        if factor is not None:
+            res = res * factor
         for e in range(group):
             lo = (h * group + e) * HEAD_DIM
             ref[:, lo : lo + HEAD_DIM] = res[e * tok : (e + 1) * tok, :].astype(BF16)
@@ -231,26 +233,46 @@
     for h in range(kv):
         lo = h * HEAD_DIM
         x = 2 * h
-        for t in range(1, hops + 1):
+        more = h + 1 < kv
+        top = score(h, 0, jnp.full((1, cols), -1e30, F32))
+        if h == 0:
+            arrive(x, 1)
+            start_own(x + 1)
+        for t in range(2, hops + 1):
             arrive(x, t)
+        if h == 0:
+            arrive(x + 1, 1)
+            if more:
+                start_own(x + 2)
+        if h > 0:
+            for t in range(hops - 1, 0, -1):
+                chain_step(x - 2, t, dk_ref, lo - HEAD_DIM)
+        arrive_sib(x)
+        for r in range(1, slots):
+            top = score(h, r, top)
+        probs(top)
+        part_sums(x + 1, p_ref, g2[h])
+        chain_step(x + 1, hops, dv_ref, lo)
+        if more:
+            arrive(x + 2, 1)
+            start_own(x + 3)
+        if h > 0:
+            chain_step(x - 2, 0, dk_ref, lo - HEAD_DIM)
+        for t in range(2, hops + 1):
             arrive(x + 1, t)
-            if t == 1 and h + 1 < kv:
-                start_own(x + 2)
-                start_own(x + 3)
-        arrive_sib(x)
-        stage_probs(h)
-        part_sums(x + 1, p_ref, g2[h])
         arrive_sib(x + 1)
-        chain_step(x + 1, hops, dv_ref, lo)
-        stage_scores(h)
-        emit(o_ref, h, p_ref[...], win[x + 1])
-        p_ref[...] = dp_ref[...].astype(BF16)
-        part_sums(x, p_ref, q2[h])
+        for t in range(hops - 1, 0, -1):
+            chain_step(x + 1, t, dv_ref, lo)
+        dscores(h)
+        part_sums(x, ds_ref, q2[h])
         chain_step(x, hops, dk_ref, lo)
-        emit(dq_ref, h, p_ref[...], win[x])
-        for t in range(hops - 1, -1, -1):
-            chain_step(x + 1, t, dv_ref, lo)
-            chain_step(x, t, dk_ref, lo)
+        chain_step(x + 1, 0, dv_ref, lo)
+        if more:
+            arrive(x + 3, 1)
+        emit(o_ref, h, p_ref[...], win[x + 1], None)
+        emit(dq_ref, h, ds_ref[...], win[x], scale)
+    for t in range(hops - 1, -1, -1):
+        chain_step(2 * kv - 2, t, dk_ref, (kv - 1) * HEAD_DIM)
     for x in range(2 * kv):
         finish_sends(x)
 
@@ -274,7 +296,7 @@
             jax.ShapeDtypeStruct(keys.shape[1:], BF16),
             jax.ShapeDtypeStruct(keys.shape[1:], BF16),
         ),
-        in_specs=[pl.BlockSpec(memory_space=pltpu.SMEM)] + [spec] * 4,
+        in_specs=[pl.BlockSpec(memory_space=pltpu.SMEM)] + [pl.BlockSpec(memory_space=pl.ANY)] * 4,
         out_specs=(spec,) * 4,
         scratch_shapes=[
             pltpu.VMEM((chunks, slots) + tile, BF16),
@@ -283,11 +305,17 @@
             pltpu.VMEM((slots * tok, cols), F32),
             pltpu.VMEM((slots * tok, cols), BF16),
             pltpu.VMEM((slots * tok, cols), F32),
+            pltpu.VMEM((slots * tok, cols), BF16),
             pltpu.VMEM((chunks, hops + 1) + tile, F32),
             pltpu.VMEM((chunks, hops) + tile, BF16),
             pltpu.VMEM((chunks, hops) + tile, BF16),
             pltpu.VMEM((chunks, hops) + tile, BF16),
             pltpu.VMEM((chunks, hops) + tile, BF16),
+        ]
+        + [
+            pltpu.SemaphoreType.DMA((chunks,)),
+            pltpu.SemaphoreType.DMA((kv, cols // tok)),
+            pltpu.SemaphoreType.DMA((kv, cols // tok)),
         ]
         + [dma] * 8,
         compiler_params=pltpu.CompilerParams(

time: 69.8 us -> 61.1 us (0.88)
  Pallas kernels: 61.3 us -> 52.5 us
    pallas_call x1, Pallas kernels: 61.3 us -> 52.5 us  [body(): pl.pallas_call(functools.partial(kernel, n, hops), out_shape=(jax.ShapeDt...]
where the time goes in v1:
time: 61.1 us; the launch traced here: 60.8 us
  Pallas kernels  52.5 us (86%)
  local copies, waits for them, and re-layouts  7.62 us (12%)
  between operations  0.65 us (1%)
    pallas_call x1, Pallas kernels, body(): pl.pallas_call(functools.partial(kernel, n, hops), out_shape=(jax.ShapeDt...  52.5 us
    unnamed x14, local copies, waits for them, and re-layouts  7.62 us

profile of v1, /device:TPU:0, one launch (start us, length us, event | category | flops | bytes accessed | tf_op | source)
XLA Modules:
  0.0 60.8 jit_solution(12833156667620872708)
XLA Ops:
  0.6 0.0 copy-start.4
  0.6 0.6 %copy-done.4 = s32[4]{0:T(128)S(1)} copy-done((s32[4]{0:T(128)S(1)}, s32[4]{0:T(128)}, u32[]{:S(2)}) %copy-start.4) | copy-done | bytes 40
  1.3 0.0 copy-start
  1.3 1.0 %copy-done = bf16[1,256,1024]{2,1,0:T(8,128)(2,1)S(1)} copy-done((bf16[1,256,1024]{2,1,0:T(8,128)(2,1)S(1)}, bf16[1,256,1024]{2,1,0:T(8,128)(2,1)}, u32[]{:S(2)}) %copy-start) | copy-done | bytes 524312
  2.3 0.0 copy-start.1
  2.3 1.0 %copy-done.1 = bf16[1,256,1024]{2,1,0:T(8,128)(2,1)S(1)} copy-done((bf16[1,256,1024]{2,1,0:T(8,128)(2,1)S(1)}, bf16[1,256,1024]{2,1,0:T(8,128)(2,1)}, u32[]{:S(2)}) %copy-start.1) | copy-done | bytes 524312
  3.4 0.0 copy-start.2
  3.4 0.9 %copy-done.2 = bf16[1,256,512]{2,1,0:T(8,128)(2,1)S(1)} copy-done((bf16[1,256,512]{2,1,0:T(8,128)(2,1)S(1)}, bf16[1,256,512]{2,1,0:T(8,128)(2,1)}, u32[]{:S(2)}) %copy-start.2) | copy-done | bytes 262168
  4.3 0.0 copy-start.3
  4.3 0.9 %copy-done.3 = bf16[1,256,512]{2,1,0:T(8,128)(2,1)S(1)} copy-done((bf16[1,256,512]{2,1,0:T(8,128)(2,1)S(1)}, bf16[1,256,512]{2,1,0:T(8,128)(2,1)}, u32[]{:S(2)}) %copy-start.3) | copy-done | bytes 262168
  5.3 52.5 %shard_map.84 = (bf16[256,1024]{1,0:T(8,128)(2,1)S(1)}, bf16[256,1024]{1,0:T(8,128)(2,1)S(1)}, bf16[256,512]{1,0:T(8,128)(2,1)S(1)}, bf16[256,512]{1,0:T(8,128)(2,1)S(1)}) custom-call(s32[4]{0:T(128)S(1)} %copy-done.4, bf16[256,1024]{1,0:T(8,128)(2,1)S(1)} %bitcast.8, bf16[256,512]{1,0:T(8,128)(2,1)S(1)} %bitcast.14, bf16[256,512]{1,0:T(8,128)(2,1)S(1)} %bitcast.15, ...), custom_call_target="tpu_custom_call" | custom-call | tf_op jit(solution)/shard_map/pallas_call | solution.py:291
  57.8 0.8 %copy.13 = bf16[1,256,1024]{2,1,0:T(8,128)(2,1)} copy(bf16[1,256,1024]{2,1,0:T(8,128)(2,1)S(1)} %bitcast.11) | data formatting | bytes 1048576
  58.6 0.8 %copy.14 = bf16[1,256,1024]{2,1,0:T(8,128)(2,1)} copy(bf16[1,256,1024]{2,1,0:T(8,128)(2,1)S(1)} %bitcast.10) | data formatting | bytes 1048576
  59.4 0.7 %copy.15 = bf16[1,256,512]{2,1,0:T(8,128)(2,1)} copy(bf16[1,256,512]{2,1,0:T(8,128)(2,1)S(1)} %bitcast.13) | data formatting | bytes 524288
  60.1 0.7 %copy.16 = bf16[1,256,512]{2,1,0:T(8,128)(2,1)} copy(bf16[1,256,512]{2,1,0:T(8,128)(2,1)S(1)} %bitcast.12) | data formatting | bytes 524288
Async XLA Ops:
  0.6 0.7 %copy-start.4 = (s32[4]{0:T(128)S(1)}, s32[4]{0:T(128)}, u32[]{:S(2)}) copy-start(s32[4]{0:T(128)} %docs_ref.1) | copy-start | bytes 52
  1.3 1.0 %copy-start = (bf16[1,256,1024]{2,1,0:T(8,128)(2,1)S(1)}, bf16[1,256,1024]{2,1,0:T(8,128)(2,1)}, u32[]{:S(2)}) copy-start(bf16[1,256,1024]{2,1,0:T(8,128)(2,1)} %param.6) | copy-start | bytes 1572868
  2.3 1.0 %copy-start.1 = (bf16[1,256,1024]{2,1,0:T(8,128)(2,1)S(1)}, bf16[1,256,1024]{2,1,0:T(8,128)(2,1)}, u32[]{:S(2)}) copy-start(bf16[1,256,1024]{2,1,0:T(8,128)(2,1)} %param.9) | copy-start | bytes 1572868
  3.4 0.9 %copy-start.2 = (bf16[1,256,512]{2,1,0:T(8,128)(2,1)S(1)}, bf16[1,256,512]{2,1,0:T(8,128)(2,1)}, u32[]{:S(2)}) copy-start(bf16[1,256,512]{2,1,0:T(8,128)(2,1)} %param.7) | copy-start | bytes 786436
  4.3 0.9 %copy-start.3 = (bf16[1,256,512]{2,1,0:T(8,128)(2,1)S(1)}, bf16[1,256,512]{2,1,0:T(8,128)(2,1)}, u32[]{:S(2)}) copy-start(bf16[1,256,512]{2,1,0:T(8,128)(2,1)} %param.8) | copy-start | bytes 786436

commit v2 on v1

--- a/solution.py
+++ b/solution.py
@@ -158,6 +158,7 @@
             load_rows(g_ref, g2, lg, h, e).start()
     pl.semaphore_wait(barrier, 3)
     start_own(0)
+    start_own(1)
 
     for h in range(kv):
         for e in range(group):
@@ -197,29 +198,36 @@
             e = jnp.exp(s_ref[rows(r), :] - top)
             s_ref[rows(r), :] = e
             total = total + jnp.sum(e, axis=0, keepdims=True)
-        inv = 1.0 / total
-        for r in range(slots):
-            prob = s_ref[rows(r), :] * inv
-            s_ref[rows(r), :] = prob
-            p_ref[rows(r), :] = prob.astype(BF16)
-
-    def part_sums(x, lhs, rhs):
-        order = list(range(slots - 2, 0, -2)) + list(range(slots - 1, -1, -2))
-        for r in order:
-            part = jnp.dot(lhs[rows(r), :], rhs, preferred_element_type=F32)
+        return 1.0 / total
+
+    def normalise(h, r, inv):
+        prob = s_ref[rows(r), :] * inv
+        s_ref[rows(r), :] = prob
+        p_ref[h, rows(r), :] = prob.astype(BF16)
+
+    def part_sums(x, make, lhs, rhs, out_ref, lo):
+        far = [slots - 2, slots - 1]
+        rest = list(range(slots - 4, 0, -2)) + list(range(slots - 3, -1, -2))
+        for r in far + rest:
+            make(r)
+            part = jnp.dot(lhs[x // 2, rows(r), :], rhs, preferred_element_type=F32)
             if r % 2:
                 send_odd(x, r // 2, part)
             else:
                 acc[x, r // 2] = part
-
-    def dscores(h):
+            if r == slots - 1:
+                chain_step(x, hops, out_ref, lo)
+
+    def deltas(h):
         delta = jnp.zeros((1, cols), F32)
         for r in range(slots):
             dp = lax.dot_general(win[2 * h + 1, r], g2[h], CONTRACT_LAST, preferred_element_type=F32)
             dp_ref[rows(r), :] = dp
             delta = delta + jnp.sum(dp * s_ref[rows(r), :], axis=0, keepdims=True)
-        for r in range(slots):
-            ds_ref[rows(r), :] = (s_ref[rows(r), :] * (dp_ref[rows(r), :] - delta)).astype(BF16)
+        return delta
+
+    def dscore(h, r, delta):
+        ds_ref[h, rows(r), :] = (s_ref[rows(r), :] * (dp_ref[rows(r), :] - delta)).astype(BF16)
 
     def emit(ref, h, weights, source, factor):
         whole = source.reshape(slots * tok, HEAD_DIM)
@@ -237,42 +245,41 @@
         top = score(h, 0, jnp.full((1, cols), -1e30, F32))
         if h == 0:
             arrive(x, 1)
-            start_own(x + 1)
-        for t in range(2, hops + 1):
-            arrive(x, t)
-        if h == 0:
             arrive(x + 1, 1)
             if more:
                 start_own(x + 2)
+                start_own(x + 3)
+        for t in range(2, hops + 1):
+            arrive(x, t)
         if h > 0:
             for t in range(hops - 1, 0, -1):
                 chain_step(x - 2, t, dk_ref, lo - HEAD_DIM)
         arrive_sib(x)
         for r in range(1, slots):
             top = score(h, r, top)
-        probs(top)
-        part_sums(x + 1, p_ref, g2[h])
-        chain_step(x + 1, hops, dv_ref, lo)
+        inv = probs(top)
+        part_sums(x + 1, functools.partial(normalise, h, inv=inv), p_ref, g2[h], dv_ref, lo)
         if more:
             arrive(x + 2, 1)
-            start_own(x + 3)
         if h > 0:
             chain_step(x - 2, 0, dk_ref, lo - HEAD_DIM)
         for t in range(2, hops + 1):
             arrive(x + 1, t)
         arrive_sib(x + 1)
+        delta = deltas(h)
         for t in range(hops - 1, 0, -1):
             chain_step(x + 1, t, dv_ref, lo)
-        dscores(h)
-        part_sums(x, ds_ref, q2[h])
-        chain_step(x, hops, dk_ref, lo)
+        part_sums(x, functools.partial(dscore, h, delta=delta), ds_ref, q2[h], dk_ref, lo)
         chain_step(x + 1, 0, dv_ref, lo)
         if more:
             arrive(x + 3, 1)
-        emit(o_ref, h, p_ref[...], win[x + 1], None)
-        emit(dq_ref, h, ds_ref[...], win[x], scale)
+    for h in range(kv):
+        emit(o_ref, h, p_ref[h], win[2 * h + 1], None)
     for t in range(hops - 1, -1, -1):
         chain_step(2 * kv - 2, t, dk_ref, (kv - 1) * HEAD_DIM)
+        if t == hops - 1:
+            for h in range(kv):
+                emit(dq_ref, h, ds_ref[h], win[2 * h], scale)
     for x in range(2 * kv):
         finish_sends(x)
 
@@ -303,9 +310,9 @@
             pltpu.VMEM((kv, cols, HEAD_DIM), BF16),
             pltpu.VMEM((kv, cols, HEAD_DIM), BF16),
             pltpu.VMEM((slots * tok, cols), F32),
-            pltpu.VMEM((slots * tok, cols), BF16),
+            pltpu.VMEM((kv, slots * tok, cols), BF16),
             pltpu.VMEM((slots * tok, cols), F32),
-            pltpu.VMEM((slots * tok, cols), BF16),
+            pltpu.VMEM((kv, slots * tok, cols), BF16),
             pltpu.VMEM((chunks, hops + 1) + tile, F32),
             pltpu.VMEM((chunks, hops) + tile, BF16),
             pltpu.VMEM((chunks, hops) + tile, BF16),

time: 61.1 us -> 55.3 us (0.905)
  Pallas kernels: 52.5 us -> 46.7 us
    pallas_call x1, Pallas kernels: 52.5 us -> 46.7 us  [body(): pl.pallas_call(functools.partial(kernel, n, hops), out_shape=(jax.ShapeDt...]
where the time goes in v2:
time: 55.3 us; the launch traced here: 55 us
  Pallas kernels  46.7 us (84%)
  local copies, waits for them, and re-layouts  7.62 us (14%)
  between operations  0.65 us (1%)
    pallas_call x1, Pallas kernels, body(): pl.pallas_call(functools.partial(kernel, n, hops), out_shape=(jax.ShapeDt...  46.7 us
    unnamed x14, local copies, waits for them, and re-layouts  7.62 us

profile of v2, /device:TPU:0, one launch (start us, length us, event | category | flops | bytes accessed | tf_op | source)
XLA Modules:
  0.0 55.0 jit_solution(9515245991664815003)
XLA Ops:
  0.6 0.0 copy-start.4
  0.6 0.6 %copy-done.4 = s32[4]{0:T(128)S(1)} copy-done((s32[4]{0:T(128)S(1)}, s32[4]{0:T(128)}, u32[]{:S(2)}) %copy-start.4) | copy-done | bytes 40
  1.3 0.0 copy-start
  1.3 1.0 %copy-done = bf16[1,256,1024]{2,1,0:T(8,128)(2,1)S(1)} copy-done((bf16[1,256,1024]{2,1,0:T(8,128)(2,1)S(1)}, bf16[1,256,1024]{2,1,0:T(8,128)(2,1)}, u32[]{:S(2)}) %copy-start) | copy-done | bytes 524312
  2.3 0.0 copy-start.1
  2.3 1.0 %copy-done.1 = bf16[1,256,1024]{2,1,0:T(8,128)(2,1)S(1)} copy-done((bf16[1,256,1024]{2,1,0:T(8,128)(2,1)S(1)}, bf16[1,256,1024]{2,1,0:T(8,128)(2,1)}, u32[]{:S(2)}) %copy-start.1) | copy-done | bytes 524312
  3.4 0.0 copy-start.2
  3.4 0.9 %copy-done.2 = bf16[1,256,512]{2,1,0:T(8,128)(2,1)S(1)} copy-done((bf16[1,256,512]{2,1,0:T(8,128)(2,1)S(1)}, bf16[1,256,512]{2,1,0:T(8,128)(2,1)}, u32[]{:S(2)}) %copy-start.2) | copy-done | bytes 262168
  4.3 0.0 copy-start.3
  4.3 0.9 %copy-done.3 = bf16[1,256,512]{2,1,0:T(8,128)(2,1)S(1)} copy-done((bf16[1,256,512]{2,1,0:T(8,128)(2,1)S(1)}, bf16[1,256,512]{2,1,0:T(8,128)(2,1)}, u32[]{:S(2)}) %copy-start.3) | copy-done | bytes 262168
  5.3 46.7 %shard_map.84 = (bf16[256,1024]{1,0:T(8,128)(2,1)S(1)}, bf16[256,1024]{1,0:T(8,128)(2,1)S(1)}, bf16[256,512]{1,0:T(8,128)(2,1)S(1)}, bf16[256,512]{1,0:T(8,128)(2,1)S(1)}) custom-call(s32[4]{0:T(128)S(1)} %copy-done.4, bf16[256,1024]{1,0:T(8,128)(2,1)S(1)} %bitcast.8, bf16[256,512]{1,0:T(8,128)(2,1)S(1)} %bitcast.14, bf16[256,512]{1,0:T(8,128)(2,1)S(1)} %bitcast.15, ...), custom_call_target="tpu_custom_call" | custom-call | tf_op jit(solution)/shard_map/pallas_call | solution.py:298
  52.0 0.8 %copy.13 = bf16[1,256,1024]{2,1,0:T(8,128)(2,1)} copy(bf16[1,256,1024]{2,1,0:T(8,128)(2,1)S(1)} %bitcast.11) | data formatting | bytes 1048576
  52.8 0.8 %copy.14 = bf16[1,256,1024]{2,1,0:T(8,128)(2,1)} copy(bf16[1,256,1024]{2,1,0:T(8,128)(2,1)S(1)} %bitcast.10) | data formatting | bytes 1048576
  53.6 0.7 %copy.15 = bf16[1,256,512]{2,1,0:T(8,128)(2,1)} copy(bf16[1,256,512]{2,1,0:T(8,128)(2,1)S(1)} %bitcast.13) | data formatting | bytes 524288
  54.3 0.7 %copy.16 = bf16[1,256,512]{2,1,0:T(8,128)(2,1)} copy(bf16[1,256,512]{2,1,0:T(8,128)(2,1)S(1)} %bitcast.12) | data formatting | bytes 524288
Async XLA Ops:
  0.6 0.7 %copy-start.4 = (s32[4]{0:T(128)S(1)}, s32[4]{0:T(128)}, u32[]{:S(2)}) copy-start(s32[4]{0:T(128)} %docs_ref.1) | copy-start | bytes 52
  1.3 1.0 %copy-start = (bf16[1,256,1024]{2,1,0:T(8,128)(2,1)S(1)}, bf16[1,256,1024]{2,1,0:T(8,128)(2,1)}, u32[]{:S(2)}) copy-start(bf16[1,256,1024]{2,1,0:T(8,128)(2,1)} %param.6) | copy-start | bytes 1572868
  2.3 1.0 %copy-start.1 = (bf16[1,256,1024]{2,1,0:T(8,128)(2,1)S(1)}, bf16[1,256,1024]{2,1,0:T(8,128)(2,1)}, u32[]{:S(2)}) copy-start(bf16[1,256,1024]{2,1,0:T(8,128)(2,1)} %param.9) | copy-start | bytes 1572868
  3.4 0.9 %copy-start.2 = (bf16[1,256,512]{2,1,0:T(8,128)(2,1)S(1)}, bf16[1,256,512]{2,1,0:T(8,128)(2,1)}, u32[]{:S(2)}) copy-start(bf16[1,256,512]{2,1,0:T(8,128)(2,1)} %param.7) | copy-start | bytes 786436
  4.3 0.9 %copy-start.3 = (bf16[1,256,512]{2,1,0:T(8,128)(2,1)S(1)}, bf16[1,256,512]{2,1,0:T(8,128)(2,1)}, u32[]{:S(2)}) copy-start(bf16[1,256,512]{2,1,0:T(8,128)(2,1)} %param.8) | copy-start | bytes 786436

commit v3 on v2

--- a/solution.py
+++ b/solution.py
@@ -267,9 +267,9 @@
             arrive(x + 1, t)
         arrive_sib(x + 1)
         delta = deltas(h)
+        part_sums(x, functools.partial(dscore, h, delta=delta), ds_ref, q2[h], dk_ref, lo)
         for t in range(hops - 1, 0, -1):
             chain_step(x + 1, t, dv_ref, lo)
-        part_sums(x, functools.partial(dscore, h, delta=delta), ds_ref, q2[h], dk_ref, lo)
         chain_step(x + 1, 0, dv_ref, lo)
         if more:
             arrive(x + 3, 1)

time: 55.3 us -> 60.6 us (1.096)
  Pallas kernels: 46.7 us -> 52.1 us
    pallas_call x1, Pallas kernels: 46.7 us -> 52.1 us  [body(): pl.pallas_call(functools.partial(kernel, n, hops), out_shape=(jax.ShapeDt...]
where the time goes in v3:
time: 60.6 us; the launch traced here: 60.4 us
  Pallas kernels  52.1 us (86%)
  local copies, waits for them, and re-layouts  7.62 us (13%)
  between operations  0.65 us (1%)
    pallas_call x1, Pallas kernels, body(): pl.pallas_call(functools.partial(kernel, n, hops), out_shape=(jax.ShapeDt...  52.1 us
    unnamed x14, local copies, waits for them, and re-layouts  7.62 us

profile of v3, /device:TPU:0, one launch (start us, length us, event | category | flops | bytes accessed | tf_op | source)
XLA Modules:
  0.0 60.4 jit_solution(11272316877098413540)
XLA Ops:
  0.6 0.0 copy-start.4
  0.6 0.6 %copy-done.4 = s32[4]{0:T(128)S(1)} copy-done((s32[4]{0:T(128)S(1)}, s32[4]{0:T(128)}, u32[]{:S(2)}) %copy-start.4) | copy-done | bytes 40
  1.3 0.0 copy-start
  1.3 1.0 %copy-done = bf16[1,256,1024]{2,1,0:T(8,128)(2,1)S(1)} copy-done((bf16[1,256,1024]{2,1,0:T(8,128)(2,1)S(1)}, bf16[1,256,1024]{2,1,0:T(8,128)(2,1)}, u32[]{:S(2)}) %copy-start) | copy-done | bytes 524312
  2.3 0.0 copy-start.1
  2.3 1.0 %copy-done.1 = bf16[1,256,1024]{2,1,0:T(8,128)(2,1)S(1)} copy-done((bf16[1,256,1024]{2,1,0:T(8,128)(2,1)S(1)}, bf16[1,256,1024]{2,1,0:T(8,128)(2,1)}, u32[]{:S(2)}) %copy-start.1) | copy-done | bytes 524312
  3.4 0.0 copy-start.2
  3.4 0.9 %copy-done.2 = bf16[1,256,512]{2,1,0:T(8,128)(2,1)S(1)} copy-done((bf16[1,256,512]{2,1,0:T(8,128)(2,1)S(1)}, bf16[1,256,512]{2,1,0:T(8,128)(2,1)}, u32[]{:S(2)}) %copy-start.2) | copy-done | bytes 262168
  4.3 0.0 copy-start.3
  4.3 0.9 %copy-done.3 = bf16[1,256,512]{2,1,0:T(8,128)(2,1)S(1)} copy-done((bf16[1,256,512]{2,1,0:T(8,128)(2,1)S(1)}, bf16[1,256,512]{2,1,0:T(8,128)(2,1)}, u32[]{:S(2)}) %copy-start.3) | copy-done | bytes 262168
  5.3 52.1 %shard_map.84 = (bf16[256,1024]{1,0:T(8,128)(2,1)S(1)}, bf16[256,1024]{1,0:T(8,128)(2,1)S(1)}, bf16[256,512]{1,0:T(8,128)(2,1)S(1)}, bf16[256,512]{1,0:T(8,128)(2,1)S(1)}) custom-call(s32[4]{0:T(128)S(1)} %copy-done.4, bf16[256,1024]{1,0:T(8,128)(2,1)S(1)} %bitcast.8, bf16[256,512]{1,0:T(8,128)(2,1)S(1)} %bitcast.14, bf16[256,512]{1,0:T(8,128)(2,1)S(1)} %bitcast.15, ...), custom_call_target="tpu_custom_call" | custom-call | tf_op jit(solution)/shard_map/pallas_call | solution.py:298
  57.4 0.8 %copy.13 = bf16[1,256,1024]{2,1,0:T(8,128)(2,1)} copy(bf16[1,256,1024]{2,1,0:T(8,128)(2,1)S(1)} %bitcast.11) | data formatting | bytes 1048576
  58.2 0.8 %copy.14 = bf16[1,256,1024]{2,1,0:T(8,128)(2,1)} copy(bf16[1,256,1024]{2,1,0:T(8,128)(2,1)S(1)} %bitcast.10) | data formatting | bytes 1048576
  59.0 0.7 %copy.15 = bf16[1,256,512]{2,1,0:T(8,128)(2,1)} copy(bf16[1,256,512]{2,1,0:T(8,128)(2,1)S(1)} %bitcast.13) | data formatting | bytes 524288
  59.7 0.7 %copy.16 = bf16[1,256,512]{2,1,0:T(8,128)(2,1)} copy(bf16[1,256,512]{2,1,0:T(8,128)(2,1)S(1)} %bitcast.12) | data formatting | bytes 524288
Async XLA Ops:
  0.6 0.7 %copy-start.4 = (s32[4]{0:T(128)S(1)}, s32[4]{0:T(128)}, u32[]{:S(2)}) copy-start(s32[4]{0:T(128)} %docs_ref.1) | copy-start | bytes 52
  1.3 1.0 %copy-start = (bf16[1,256,1024]{2,1,0:T(8,128)(2,1)S(1)}, bf16[1,256,1024]{2,1,0:T(8,128)(2,1)}, u32[]{:S(2)}) copy-start(bf16[1,256,1024]{2,1,0:T(8,128)(2,1)} %param.6) | copy-start | bytes 1572868
  2.3 1.0 %copy-start.1 = (bf16[1,256,1024]{2,1,0:T(8,128)(2,1)S(1)}, bf16[1,256,1024]{2,1,0:T(8,128)(2,1)}, u32[]{:S(2)}) copy-start(bf16[1,256,1024]{2,1,0:T(8,128)(2,1)} %param.9) | copy-start | bytes 1572868
  3.4 0.9 %copy-start.2 = (bf16[1,256,512]{2,1,0:T(8,128)(2,1)S(1)}, bf16[1,256,512]{2,1,0:T(8,128)(2,1)}, u32[]{:S(2)}) copy-start(bf16[1,256,512]{2,1,0:T(8,128)(2,1)} %param.7) | copy-start | bytes 786436
  4.3 0.9 %copy-start.3 = (bf16[1,256,512]{2,1,0:T(8,128)(2,1)S(1)}, bf16[1,256,512]{2,1,0:T(8,128)(2,1)}, u32[]{:S(2)}) copy-start(bf16[1,256,512]{2,1,0:T(8,128)(2,1)} %param.8) | copy-start | bytes 786436
